TPU v7x, 128 devices: a whole 4x4x4 slice. The times are simulated.
128 devices in a mesh: state: 4 (over z_hi, core), row: 32 (over z_lo, x, y).
Axes of the slice: x: 4, y: 4, z: 4 (z_hi: 2, z_lo: 2; z = z_hi * 2 + z_lo), core: 2. Of those that a mesh axis runs over, the one named last changes fastest.
Arguments:
- vectors: bfloat16 [131072, 512], P('row', 'state'), as said below
- active: int32 [8], replicated, may hold values 0 or 1
Outputs:
- orthonormal: bfloat16 [131072, 512], P('row', 'state')
Inputs may be any that keep to these rules, and one draw needn't show every extreme that they name: Each row and each column of vectors has its own scale.
All inputs are finite; a program needn't handle non-finite values.
Results may differ from a plain program's by a relative error of at most 0.00096.
Values may be sent and summed in bfloat16 or wider, within the bound.
A program may use at most 64 MiB of HBM per device.

v0:
```python
import jax
import jax.numpy as jnp
from jax import lax
from jax.sharding import PartitionSpec as P

VECS = 64
ITERS = 5


def newton_schulz(gram_matrix, total_rows):
    identity = jnp.eye(gram_matrix.shape[0], dtype=jnp.float32)
    frob_norm = jnp.sqrt(jnp.sum(gram_matrix * gram_matrix))
    current = gram_matrix / frob_norm
    inverse = identity
    for repeat in range(ITERS):
        newton_step = 0.5 * (
            3.0 * identity - jnp.dot(inverse, current, precision=lax.Precision.HIGHEST)
        )
        current = jnp.dot(current, newton_step, precision=lax.Precision.HIGHEST)
        inverse = jnp.dot(newton_step, inverse, precision=lax.Precision.HIGHEST)
    return (inverse * jnp.sqrt(total_rows / frob_norm)).astype(jnp.bfloat16)


def cross_product(left_block, right_block):
    return lax.dot_general(
        left_block, right_block, (((0,), (0,)), ((), ())), preferred_element_type=jnp.float32
    )


def shards(vectors, active):
    block_width = vectors.shape[1]
    total_rows = vectors.shape[0] * lax.axis_size("row")
    start_col = lax.axis_index("state") * block_width
    flag_all = jnp.repeat(active.astype(jnp.float32), VECS)
    flag_cols = lax.dynamic_slice_in_dim(flag_all, start_col, block_width, 0)
    masked = vectors * flag_cols.astype(jnp.bfloat16)
    gathered = lax.all_gather(masked, "state", axis=1, tiled=True)
    gram_matrix = cross_product(gathered, gathered)
    gram_matrix = lax.psum(gram_matrix, "row")
    gram_matrix = gram_matrix + jnp.diag((1.0 - flag_all) * total_rows)
    factor = newton_schulz(gram_matrix, total_rows)
    my_factor = lax.dynamic_slice_in_dim(factor, start_col, block_width, 1)
    result = jnp.dot(gathered, my_factor, preferred_element_type=jnp.float32)
    result = result + (1.0 - flag_cols) * vectors.astype(jnp.float32)
    return result.astype(jnp.bfloat16)


def solution(mesh):
    in_specs = (P("row", "state"), P())
    out_specs = P("row", "state")
    return jax.shard_map(shards, mesh=mesh, in_specs=in_specs, out_specs=out_specs, check_vma=False)
```

profile of v0, /device:TPU:0, one launch (start us, length us, event | category | flops | bytes accessed | tf_op | source)
XLA Modules:
  0.0 406.8 jit_solution(8900050890068867705)
XLA Ops:
  6.5 0.0 all-gather.2.cloned.1.call-start
  6.5 0.7 convert_element_type.16
  7.2 0.1 broadcast_in_dim.21
  7.3 0.1 reshape.11
  7.3 0.1 dynamic_slice.15
  7.4 2.3 broadcast_multiply_fusion
  9.7 0.0 all-gather.2.cloned.1.call-update
  9.7 0.0 all-reduce.2.cloned.1.call-start
  9.8 41.8 %all-gather.2.cloned.1.call-done = bf16[4096,512]{1,0:T(8,128)(2,1)} async-done(((bf16[4096,128]{1,0:T(8,128)(2,1)}), bf16[4096,512]{1,0:T(8,128)(2,1)}) %all-gather.2.cloned.1.call-update) | async-done | bytes 4194320 | tf_op jit(solution)/shard_map/all_gather | solution.py:37
  51.5 6.8 %fusion.15 = f32[512,512]{1,0:T(8,128)} fusion(bf16[4096,512]{1,0:T(8,128)(2,1)} %all-gather.2.cloned.1.call-done), kind=kOutput, calls=%fused_computation.26 | convolution fusion | flops 2147483648 | bytes 5242880 | tf_op jit(solution)/shard_map/dot_general | solution.py:25
  58.3 0.0 all-reduce.2.cloned.1.call-update
  58.4 0.1 broadcast_subtract_fusion
  58.4 310.3 %all-reduce.2.cloned.1.call-done = f32[512,512]{1,0:T(8,128)} async-done(((f32[512,512]{1,0:T(8,128)}), f32[512,512]{1,0:T(8,128)}) %all-reduce.2.cloned.1.call-update) | async-done | bytes 1048592 | tf_op jit(solution)/shard_map/psum | solution.py:39
  368.8 2.2 multiply_reduce_fusion
  371.6 0.0 copy-start.2
  371.7 2.4 fusion.5
  374.1 1.0 fusion.6
  375.1 0.0 copy-done.2
  375.1 1.9 fusion.12
  377.0 1.8 fusion.1
  378.8 1.8 fusion.17
  380.7 1.8 fusion.16
  382.6 2.0 fusion.2
  384.6 1.8 fusion.19
  386.5 1.8 fusion.18
  388.3 1.9 fusion.3
  390.2 1.8 fusion.20
  392.0 0.0 copy-start.1
  392.0 1.8 fusion.21
  394.0 0.0 copy-start
  394.0 1.9 fusion.4
  395.9 1.9 fusion.22
  397.7 0.0 copy-done.1
  397.7 0.0 copy-done
  397.7 2.2 fusion
  (1 shorter events, 0.0 us)
Async XLA Ops:
  6.5 45.0 %all-gather.2.cloned.1.call-start = ((), (), s32[]{:S(2)}) async-start(), calls=%async_computation | async-start | bytes 5242880 | tf_op jit(solution)/shard_map/all_gather | solution.py:37
  9.7 359.1 %all-reduce.2.cloned.1.call-start = ((), (), s32[]{:S(2)}) async-start(), calls=%async_computation.1 | async-start | bytes 2097152 | tf_op jit(solution)/shard_map/psum | solution.py:39
  371.6 3.4 copy-start.2
  392.0 5.7 %copy-start.1 = (bf16[4096,128]{1,0:T(8,128)(2,1)S(1)}, bf16[4096,128]{1,0:T(8,128)(2,1)}, u32[]{:S(2)}) copy-start(bf16[4096,128]{1,0:T(8,128)(2,1)} %param.2) | copy-start | bytes 3145732
  394.0 3.7 copy-start
Sparse Core Ops, SparseCore 0:
  9.8 41.6 all-gather.1
  58.5 310.2 all-reduce.1
where the time goes:
time: 407 us
  waiting for transfers between devices  352 us (86%)
  matrix products  34.9 us (9%)
  between operations  14.3 us (4%)
  other arithmetic  5.17 us (1%)
    psum x1, waiting for transfers between devices, shards(): gram_matrix = lax.psum(gram_matrix, 'row')  310 us
    all_gather x1, waiting for transfers between devices, shards(): gathered = lax.all_gather(masked, 'state', axis=1, tiled=True)  41.8 us
    dot_general x5, matrix products, newton_schulz(): jnp.dot(inverse, current, precision=lax.Precision.HIGHEST)  10 us
    dot_general x5, matrix products, newton_schulz(): inverse = jnp.dot(newton_step, inverse, precision=lax.Precision.HIGHEST)  8.37 us
  transfers between devices with their start and end apart: 2, of which 2 were waited for; matrix products, arithmetic and copies ran while one was open for 0% of the time, Pallas kernels for 0%

commit v1 on v0

--- a/solution.py
+++ b/solution.py
@@ -1,3 +1,4 @@
+import functools
 import jax
 import jax.numpy as jnp
 from jax import lax
@@ -5,6 +6,18 @@
 
 VECS = 64
 ITERS = 5
+
+
+def keep_up_stacks_all_on_mesh(xx, axis_no):
+    return jnp.concatenate(
+        lax.all_to_all(
+            jnp.stack([xx] * lax.psum(1, "state")), "state", split_axis=0, concat_axis=0
+        ),
+        axis_no,
+    )
+
+
+face_follow = functools.partial(keep_up_stacks_all_on_mesh, axis_no=1)
 
 
 def newton_schulz(gram_matrix, total_rows):
@@ -34,7 +47,7 @@
     flag_all = jnp.repeat(active.astype(jnp.float32), VECS)
     flag_cols = lax.dynamic_slice_in_dim(flag_all, start_col, block_width, 0)
     masked = vectors * flag_cols.astype(jnp.bfloat16)
-    gathered = lax.all_gather(masked, "state", axis=1, tiled=True)
+    gathered = face_follow(masked)
     gram_matrix = cross_product(gathered, gathered)
     gram_matrix = lax.psum(gram_matrix, "row")
     gram_matrix = gram_matrix + jnp.diag((1.0 - flag_all) * total_rows)

time: 407 us -> 421 us (1.034)
  blocking collectives: 0 us -> 54.7 us
  waiting for transfers between devices: 352 us -> 311 us
    all_to_all x0 -> x1, blocking collectives: none -> 54.7 us  [keep_up_stacks_all_on_mesh(): lax.all_to_all(jnp.stack([xx] * lax.psum(1, 'state')), 'state', split_axi...]
    all_gather x1 -> x0, waiting for transfers between devices: 41.8 us -> none  [shards(): gathered = lax.all_gather(masked, 'state', axis=1, tiled=True)]
  transfers between devices with their start and end apart: 2 -> 1, of which waited for: 2 -> 1; matrix products, arithmetic and copies ran while one was open for 0% -> 0% of each run, Pallas kernels for 0% -> 0%
where the time goes in v1:
time: 421 us
  waiting for transfers between devices  311 us (74%)
  blocking collectives  54.7 us (13%)
  matrix products  33.9 us (8%)
  between operations  14.3 us (3%)
    psum x1, waiting for transfers between devices, shards(): gram_matrix = lax.psum(gram_matrix, 'row')  311 us
    all_to_all x1, blocking collectives, keep_up_stacks_all_on_mesh(): lax.all_to_all(jnp.stack([xx] * lax.psum(1, 'state')), 'state', split_axi...  54.7 us
    dot_general x5, matrix products, newton_schulz(): jnp.dot(inverse, current, precision=lax.Precision.HIGHEST)  10 us
    dot_general x5, matrix products, newton_schulz(): inverse = jnp.dot(newton_step, inverse, precision=lax.Precision.HIGHEST)  8.6 us
  transfers between devices with their start and end apart: 1, of which 1 were waited for; matrix products, arithmetic and copies ran while one was open for 0% of the time, Pallas kernels for 0%

profile of v1, /device:TPU:0, one launch (start us, length us, event | category | flops | bytes accessed | tf_op | source)
XLA Modules:
  0.0 421.0 jit_solution(8834540852641004241)
XLA Ops:
  6.5 0.0 all-reduce.2.cloned.1.call-start
  6.5 0.7 convert_element_type.16
  7.2 0.1 broadcast_in_dim.21
  7.3 0.1 reshape.19
  7.3 0.1 dynamic_slice.15
  7.4 1.3 broadcast_multiply_fusion
  8.7 0.5 copy.3
  9.3 0.6 stack.2
  9.8 54.7 %all_to_all.5 = bf16[4,4096,128]{1,2,0:T(8,128)(2,1)S(1)} all-to-all(bf16[4,4096,128]{1,2,0:T(8,128)(2,1)S(1)} %stack.2), channel_id=1, replica_groups=mesh['state'=4,'row'=32] {'state'}, dimensions={0} | all-to-all | bytes 8388608 | tf_op jit(solution)/shard_map/all_to_all | solution.py:13
  64.5 0.0 copy-start
  64.5 1.9 copy-done
  66.5 3.3 fusion.15
  69.8 0.0 all-reduce.2.cloned.1.call-update
  69.8 0.1 broadcast_subtract_fusion
  69.9 310.5 %all-reduce.2.cloned.1.call-done = f32[512,512]{1,0:T(8,128)} async-done(((f32[512,512]{1,0:T(8,128)}), f32[512,512]{1,0:T(8,128)}) %all-reduce.2.cloned.1.call-update) | async-done | bytes 1048592 | tf_op jit(solution)/shard_map/psum | solution.py:52
  380.4 2.2 multiply_reduce_fusion
  383.3 0.0 copy-start.2
  383.3 2.4 fusion.5
  385.7 1.0 fusion.6
  386.7 0.0 copy-done.2
  386.7 1.9 fusion.12
  388.6 1.9 fusion.1
  390.5 1.8 fusion.17
  392.3 1.8 fusion.16
  394.2 2.0 fusion.2
  396.3 1.8 fusion.19
  398.1 1.8 fusion.18
  400.0 1.9 fusion.3
  401.8 1.8 fusion.21
  403.7 0.0 copy-start.1
  403.7 1.8 fusion.20
  405.6 1.9 fusion.4
  407.4 2.1 fusion.22
  409.6 0.0 copy-done.1
  409.6 4.5 %fusion = bf16[4096,128]{1,0:T(8,128)(2,1)} fusion(bf16[4096,512]{0,1:T(8,128)(2,1)} %bitcast.31, bf16[4096,128]{1,0:T(8,128)(2,1)S(1)} %copy-done.1, f32[128]{0:T(128)S(1)} %broadcast_subtract_fusion, f32[512,512]{1,0:T(8,128)S(1)} %fusion.22, s32[]{:T(128)S(6)} %select_n.9, f32[]{:T(128)S(6)} %sqrt.7), kind=kOutput, calls=%fused_computation.1 | convolution fusion | flops 539099136 | bytes 6554120 | tf_op jit(solution)/shard_map/dot_general | solution.py:56
  (1 shorter events, 0.0 us)
Async XLA Ops:
  6.5 373.9 %all-reduce.2.cloned.1.call-start = ((), (), s32[]{:S(2)}) async-start(), calls=%async_computation.1 | async-start | bytes 2097152 | tf_op jit(solution)/shard_map/psum | solution.py:52
  64.5 1.9 copy-start
  383.3 3.4 copy-start.2
  403.7 5.9 %copy-start.1 = (bf16[4096,128]{1,0:T(8,128)(2,1)S(1)}, bf16[4096,128]{1,0:T(8,128)(2,1)}, u32[]{:S(2)}) copy-start(bf16[4096,128]{1,0:T(8,128)(2,1)} %param.2) | copy-start | bytes 3145732
Sparse Core Ops, SparseCore 0:
  70.0 310.4 all-reduce.1
